TPU v7x, 32 devices: a whole 2x2x4 slice. The times are simulated.
32 devices in a mesh: row: 16 (over z, y, x), col: 2 (over core).
Axes of the slice: x: 2, y: 2, z: 4, core: 2. Of those that a mesh axis runs over, the one named last changes fastest.
Arguments:
- samples: bfloat16 [32768, 8192], P('row', 'col'), may hold values from -0.046875 to 0.046875
- targets: float32 [32768, 128], P('row'), may hold values from -6 to 6
- factor_inv: float32 [2, 4096, 4096], P('col', None, 'row'), may hold values from -1 to 1, as said below
Outputs:
- solution: float32 [8192, 128], P('col')
- residual: float32 [32768, 128], P('row')
Inputs may be any that keep to these rules, and one draw needn't show every extreme that they name: Each factor_inv[j] is lower triangular with a positive diagonal.
All inputs are finite; a program needn't handle non-finite values.
Results may differ from a plain program's by a relative error of at most 0.0039.
Values sent between devices are 32-bit elements; how exact they have to be, the bound alone decides.
A program may use at most 128 MiB of HBM per device.

v0:
```python
import jax
import jax.numpy as jnp
from jax import lax
from jax.sharding import PartitionSpec as P

ROUNDS = 3
ridge_weight = 0.5


def run_group(samples, residual, inverse, own_rows, offset, relaxation):
    solution = jnp.zeros((samples.shape[1], residual.shape[1]), jnp.float32)
    for sweep in range(ROUNDS):
        res16 = residual.astype(jnp.bfloat16)
        part_grad = jnp.einsum("rb,rk->bk", samples, res16, preferred_element_type=jnp.float32)
        own_solution = lax.dynamic_slice_in_dim(solution, offset, own_rows, 0)
        grad_own = (
            lax.psum_scatter(part_grad, "row", scatter_dimension=0, tiled=True)
            - ridge_weight * own_solution
        )
        term = jnp.dot(inverse, grad_own, precision=lax.Precision.HIGHEST)
        image = lax.psum(term, "row")
        update_own = jnp.einsum("bc,bk->ck", inverse, image, precision=lax.Precision.HIGHEST)
        update = lax.all_gather(update_own, "row", axis=0, tiled=True)
        solution = solution + relaxation * update
        change = jnp.dot(samples, update.astype(jnp.bfloat16), preferred_element_type=jnp.float32)
        residual = residual - relaxation * lax.psum(change, "col")
    return (solution, residual)


def per_device(samples, targets, factor_inv):
    inverse = factor_inv[0]
    own_rows = inverse.shape[1]
    offset = lax.axis_index("row") * own_rows
    relaxation = 1.0 / lax.axis_size("col")
    solution, residual = run_group(samples, targets, inverse, own_rows, offset, relaxation)
    return (solution, residual)


def solution(mesh):
    in_specs = (P("row", "col"), P("row", None), P("col", None, "row"))
    out_specs = (P("col", None), P("row", None))
    return jax.shard_map(
        per_device, mesh=mesh, in_specs=in_specs, out_specs=out_specs, check_vma=False
    )
```

profile of v0, /device:TPU:0, one launch (start us, length us, event | category | flops | bytes accessed | tf_op | source)
XLA Modules:
  0.0 985.5 jit_solution(3133331421541427131)
XLA Ops:
  7.2 11.9 %fusion.23 = f32[4096,128]{1,0:T(8,128)} fusion(bf16[2048,4096]{1,0:T(8,128)(2,1)} %param.3, f32[2048,128]{1,0:T(8,128)} %param.4), kind=kOutput, calls=%fused_computation.31 | convolution fusion | flops 2147745792 | bytes 19922944 | tf_op jit(solution)/shard_map/rb,rk->bk/dot_general | solution.py:14
  19.2 83.5 %reduce-scatter.4.cloned.1.call-done = f32[256,128]{1,0:T(8,128)} async-done(((f32[4096,128]{1,0:T(8,128)}), f32[256,128]{1,0:T(8,128)}) %reduce-scatter.4.cloned.1.call-update) | async-done | bytes 131088 | tf_op jit(solution)/shard_map/reduce_scatter | solution.py:17
  102.7 8.1 convolution_bitcast_fusion.4
  110.8 123.0 %all-reduce.7.cloned.1.call-done = f32[4096,128]{0,1:T(8,128)} async-done(((f32[4096,128]{0,1:T(8,128)}), f32[4096,128]{0,1:T(8,128)}) %all-reduce.7.cloned.1.call-update) | async-done | bytes 2097168 | tf_op jit(solution)/shard_map/psum | solution.py:21
  233.9 5.6 fusion.9
  240.0 60.7 %all-gather.4.cloned.1.call-done = f32[4096,128]{0,1:T(8,128)} async-done(((f32[256,128]{0,1:T(8,128)}), f32[4096,128]{0,1:T(8,128)}) %all-gather.4.cloned.1.call-update) | async-done | bytes 2097168 | tf_op jit(solution)/shard_map/all_gather | solution.py:23
  300.7 13.0 %convolution_bitcast_fusion.7 = f32[2048,128]{0,1:T(8,128)} fusion(bf16[2048,4096]{1,0:T(8,128)(2,1)} %param.3, f32[4096,128]{0,1:T(8,128)} %all-gather.4.cloned.1.call-done), kind=kOutput, calls=%fused_computation.16 | convolution fusion | flops 2148007936 | bytes 19922944 | tf_op jit(solution)/shard_map/dot_general | solution.py:25
  314.2 17.5 %all-reduce.9.cloned.1.call-done = f32[2048,128]{0,1:T(8,128)} async-done(((f32[2048,128]{0,1:T(8,128)}), f32[2048,128]{0,1:T(8,128)}) %all-reduce.9.cloned.1.call-update) | async-done | bytes 1048592 | tf_op jit(solution)/shard_map/psum | solution.py:26
  331.7 9.8 convolution_bitcast_fusion.1
  344.6 78.9 %reduce-scatter.6.cloned.1.call-done = f32[256,128]{0,1:T(8,128)} async-done(((f32[4096,128]{0,1:T(8,128)}), f32[256,128]{0,1:T(8,128)}) %reduce-scatter.6.cloned.1.call-update) | async-done | bytes 131088 | tf_op jit(solution)/shard_map/reduce_scatter | solution.py:17
  423.5 7.9 convolution_bitcast_fusion.3
  431.6 122.8 %all-reduce.11.cloned.1.call-done = f32[4096,128]{0,1:T(8,128)} async-done(((f32[4096,128]{0,1:T(8,128)}), f32[4096,128]{0,1:T(8,128)}) %all-reduce.11.cloned.1.call-update) | async-done | bytes 2097168 | tf_op jit(solution)/shard_map/psum | solution.py:21
  554.5 5.6 fusion.12
  560.1 61.2 %all-gather.6.cloned.1.call-done = f32[4096,128]{0,1:T(8,128)} async-done(((f32[256,128]{0,1:T(8,128)}), f32[4096,128]{0,1:T(8,128)}) %all-gather.6.cloned.1.call-update) | async-done | bytes 2097168 | tf_op jit(solution)/shard_map/all_gather | solution.py:23
  621.3 13.0 %convolution_bitcast_fusion.6 = f32[2048,128]{0,1:T(8,128)} fusion(bf16[2048,4096]{1,0:T(8,128)(2,1)} %param.3, f32[4096,128]{0,1:T(8,128)} %all-gather.6.cloned.1.call-done), kind=kOutput, calls=%fused_computation.15 | convolution fusion | flops 2148007936 | bytes 19922944 | tf_op jit(solution)/shard_map/dot_general | solution.py:25
  634.4 17.9 %all-reduce.13.cloned.1.call-done = f32[2048,128]{0,1:T(8,128)} async-done(((f32[2048,128]{0,1:T(8,128)}), f32[2048,128]{0,1:T(8,128)}) %all-reduce.13.cloned.1.call-update) | async-done | bytes 1048592 | tf_op jit(solution)/shard_map/psum | solution.py:26
  652.3 10.2 %convolution_bitcast_fusion = f32[4096,128]{0,1:T(8,128)} fusion(bf16[2048,4096]{1,0:T(8,128)(2,1)} %param.3, f32[2048,128]{0,1:T(8,128)} %all-reduce.13.cloned.1.call-done, f32[2048,128]{0,1:T(8,128)S(1)} %copy.5, f32[2048,128]{0,1:T(8,128)} %all-reduce.9.cloned.1.call-done), kind=kOutput, calls=%fused_computation | convolution fusion | flops 2148794368 | bytes 22020096 | tf_op jit(solution)/shard_map/rb,rk->bk/dot_general | solution.py:14
  665.9 78.6 %reduce-scatter.8.cloned.1.call-done = f32[256,128]{0,1:T(8,128)} async-done(((f32[4096,128]{0,1:T(8,128)}), f32[256,128]{0,1:T(8,128)}) %reduce-scatter.8.cloned.1.call-update) | async-done | bytes 131088 | tf_op jit(solution)/shard_map/reduce_scatter | solution.py:17
  744.5 7.9 convolution_bitcast_fusion.2
  752.6 122.8 %all-reduce.15.cloned.1.call-done = f32[4096,128]{0,1:T(8,128)} async-done(((f32[4096,128]{0,1:T(8,128)}), f32[4096,128]{0,1:T(8,128)}) %all-reduce.15.cloned.1.call-update) | async-done | bytes 2097168 | tf_op jit(solution)/shard_map/psum | solution.py:21
  875.4 5.6 fusion.15
  881.0 61.2 %all-gather.8.cloned.1.call-done = f32[4096,128]{0,1:T(8,128)} async-done(((f32[256,128]{0,1:T(8,128)}), f32[4096,128]{0,1:T(8,128)}) %all-gather.8.cloned.1.call-update) | async-done | bytes 2097168 | tf_op jit(solution)/shard_map/all_gather | solution.py:23
  942.2 13.2 %convolution_bitcast_fusion.5 = f32[2048,128]{0,1:T(8,128)} fusion(bf16[2048,4096]{1,0:T(8,128)(2,1)} %param.3, f32[4096,128]{0,1:T(8,128)} %all-gather.8.cloned.1.call-done), kind=kOutput, calls=%fused_computation.14 | convolution fusion | flops 2148007936 | bytes 19922944 | tf_op jit(solution)/shard_map/dot_general | solution.py:25
  961.9 11.5 %all-reduce.17.cloned.1.call-done = f32[2048,128]{0,1:T(8,128)} async-done(((f32[2048,128]{0,1:T(8,128)}), f32[2048,128]{0,1:T(8,128)}) %all-reduce.17.cloned.1.call-update) | async-done | bytes 1048592 | tf_op jit(solution)/shard_map/psum | solution.py:26
  (41 shorter events, 19.6 us)
Async XLA Ops:
  7.2 95.5 %reduce-scatter.4.cloned.1.call-start = ((), (), s32[]{:S(2)}) async-start(), calls=%async_computation.3 | async-start | bytes 2228224 | tf_op jit(solution)/shard_map/reduce_scatter | solution.py:17
  19.1 214.7 %all-reduce.7.cloned.1.call-start = ((), (), s32[]{:S(2)}) async-start(), calls=%async_computation.4 | async-start | bytes 4194304 | tf_op jit(solution)/shard_map/psum | solution.py:21
  110.8 190.0 %all-gather.4.cloned.1.call-start = ((), (), s32[]{:S(2)}) async-start(), calls=%async_computation.5 | async-start | bytes 2228224 | tf_op jit(solution)/shard_map/all_gather | solution.py:23
  239.5 74.4 %copy-start.4 = (f32[2048,128]{1,0:T(8,128)S(1)}, f32[2048,128]{1,0:T(8,128)}, u32[]{:S(2)}) copy-start(f32[2048,128]{1,0:T(8,128)} %param.4) | copy-start | bytes 3145732
  239.5 92.2 %all-reduce.9.cloned.1.call-start = ((), (), s32[]{:S(2)}) async-start(), calls=%async_computation.6 | async-start | bytes 2097152 | tf_op jit(solution)/shard_map/psum | solution.py:26
  313.8 109.7 %reduce-scatter.6.cloned.1.call-start = ((), (), s32[]{:S(2)}) async-start(), calls=%async_computation.7 | async-start | bytes 2228224 | tf_op jit(solution)/shard_map/reduce_scatter | solution.py:17
  341.5 1.6 copy-start
  341.5 213.0 %all-reduce.11.cloned.1.call-start = ((), (), s32[]{:S(2)}) async-start(), calls=%async_computation.8 | async-start | bytes 4194304 | tf_op jit(solution)/shard_map/psum | solution.py:21
  431.4 189.9 %all-gather.6.cloned.1.call-start = ((), (), s32[]{:S(2)}) async-start(), calls=%async_computation.9 | async-start | bytes 2228224 | tf_op jit(solution)/shard_map/all_gather | solution.py:23
  560.1 92.3 %all-reduce.13.cloned.1.call-start = ((), (), s32[]{:S(2)}) async-start(), calls=%async_computation.10 | async-start | bytes 2097152 | tf_op jit(solution)/shard_map/psum | solution.py:26
  634.4 110.2 %reduce-scatter.8.cloned.1.call-start = ((), (), s32[]{:S(2)}) async-start(), calls=%async_computation.11 | async-start | bytes 2228224 | tf_op jit(solution)/shard_map/reduce_scatter | solution.py:17
  662.5 212.9 %all-reduce.15.cloned.1.call-start = ((), (), s32[]{:S(2)}) async-start(), calls=%async_computation.12 | async-start | bytes 4194304 | tf_op jit(solution)/shard_map/psum | solution.py:21
  752.5 189.7 %all-gather.8.cloned.1.call-start = ((), (), s32[]{:S(2)}) async-start(), calls=%async_computation.13 | async-start | bytes 2228224 | tf_op jit(solution)/shard_map/all_gather | solution.py:23
  881.0 92.4 %all-reduce.17.cloned.1.call-start = ((), (), s32[]{:S(2)}) async-start(), calls=%async_computation.14 | async-start | bytes 2097152 | tf_op jit(solution)/shard_map/psum | solution.py:26
  942.2 13.2 %copy-start.2 = (f32[4096,128]{0,1:T(8,128)S(1)}, f32[4096,128]{0,1:T(8,128)}, u32[]{:S(2)}) copy-start(f32[4096,128]{0,1:T(8,128)} %multiply_add_fusion.1) | copy-start | bytes 6291460
  958.6 14.8 %copy-start.1 = (f32[2048,128]{0,1:T(8,128)S(1)}, f32[2048,128]{0,1:T(8,128)}, u32[]{:S(2)}) copy-start(f32[2048,128]{0,1:T(8,128)} %all-reduce.9.cloned.1.call-done) | copy-start | bytes 3145732
  958.6 14.8 %copy-start.3 = (f32[2048,128]{0,1:T(8,128)S(1)}, f32[2048,128]{0,1:T(8,128)}, u32[]{:S(2)}) copy-start(f32[2048,128]{0,1:T(8,128)} %all-reduce.13.cloned.1.call-done) | copy-start | bytes 3145732
Sparse Core Ops, SparseCore 0:
  19.3 83.3 reduce-scatter.3
  110.9 122.9 all-reduce.6
  239.6 61.0 all-gather.3
  313.9 17.7 all-reduce.8
  341.6 81.7 reduce-scatter.5
  431.5 122.8 all-reduce.10
  560.2 61.0 all-gather.5
  634.5 17.7 all-reduce.12
  662.6 81.8 reduce-scatter.7
  752.6 122.7 all-reduce.14
  881.1 61.0 all-gather.7
  955.6 17.7 all-reduce.16
where the time goes:
time: 994 us; the launch traced here: 986 us
  waiting for transfers between devices  840 us (85%)
  matrix products  112 us (11%)
  between operations  14.5 us (1%)
  other arithmetic  10.3 us (1%)
    psum x3, waiting for transfers between devices, run_group(): image = lax.psum(term, 'row')  369 us
    reduce_scatter x3, waiting for transfers between devices, run_group(): lax.psum_scatter(part_grad, 'row', scatter_dimension=0, tiled=True)  241 us
    all_gather x3, waiting for transfers between devices, run_group(): update = lax.all_gather(update_own, 'row', axis=0, tiled=True)  183 us
    psum x3, waiting for transfers between devices, run_group(): residual = residual - relaxation * lax.psum(change, 'col')  46.9 us
    dot_general x3, matrix products, run_group(): jnp.dot(samples, update.astype(jnp.bfloat16), preferred_element_type=jnp....  39.2 us
    dot_general x3, matrix products, run_group(): jnp.einsum('rb,rk->bk', samples, res16, preferred_element_type=jnp.float32)  31.9 us
    dot_general x3, matrix products, run_group(): term = jnp.dot(inverse, grad_own, precision=lax.Precision.HIGHEST)  23.9 us
  transfers between devices with their start and end apart: 12, of which 12 were waited for; matrix products, arithmetic and copies ran while one was open for 1% of the time, Pallas kernels for 0%

commit v1 on v0

--- a/solution.py
+++ b/solution.py
@@ -20,7 +20,18 @@
         term = jnp.dot(inverse, grad_own, precision=lax.Precision.HIGHEST)
         image = lax.psum(term, "row")
         update_own = jnp.einsum("bc,bk->ck", inverse, image, precision=lax.Precision.HIGHEST)
-        update = lax.all_gather(update_own, "row", axis=0, tiled=True)
+        size, position, extent = (lax.axis_size("row"), lax.axis_index("row"), update_own.shape[0])
+        ahead = [(i, (i + 1) % size) for i in range(size)]
+        filled = jnp.zeros(
+            (*update_own.shape[:0], size * extent, *update_own.shape[0 + 1 :]), update_own.dtype
+        )
+        carried = update_own
+        for turn in range(size):
+            holder = (position - turn) % size
+            filled = lax.dynamic_update_slice_in_dim(filled, carried, holder * extent, axis=0)
+            if turn < size - 1:
+                carried = lax.ppermute(carried, "row", ahead)
+        update = filled
         solution = solution + relaxation * update
         change = jnp.dot(samples, update.astype(jnp.bfloat16), preferred_element_type=jnp.float32)
         residual = residual - relaxation * lax.psum(change, "col")

time: 994 us -> 1210 us (1.22)
  waiting for transfers between devices: 840 us -> 1010 us
  local copies, waits for them, and re-layouts: 7.7 us -> 42 us
    ppermute x0 -> x45, waiting for transfers between devices: none -> 353 us  [run_group(): carried = lax.ppermute(carried, 'row', ahead)]
    all_gather x3 -> x0, waiting for transfers between devices: 183 us -> none  [run_group(): update = lax.all_gather(update_own, 'row', axis=0, tiled=True)]
    ppermute x0 -> x45, local copies, waits for them, and re-layouts: none -> 22.1 us  [run_group(): carried = lax.ppermute(carried, 'row', ahead)]
  transfers between devices with their start and end apart: 12 -> 54, of which waited for: 12 -> 54; matrix products, arithmetic and copies ran while one was open for 1% -> 4% of each run, Pallas kernels for 0% -> 0%
where the time goes in v1:
time: 1210 us; the launch traced here: 1200 us
  waiting for transfers between devices  1010 us (83%)
  matrix products  117 us (10%)
  local copies, waits for them, and re-layouts  42 us (3%)
  between operations  15.3 us (1%)
    psum x3, waiting for transfers between devices, run_group(): image = lax.psum(term, 'row')  369 us
    ppermute x45, waiting for transfers between devices, run_group(): carried = lax.ppermute(carried, 'row', ahead)  353 us
    reduce_scatter x3, waiting for transfers between devices, run_group(): lax.psum_scatter(part_grad, 'row', scatter_dimension=0, tiled=True)  243 us
    psum x3, waiting for transfers between devices, run_group(): residual = residual - relaxation * lax.psum(change, 'col')  41.9 us
    dot_general x3, matrix products, run_group(): jnp.einsum('rb,rk->bk', samples, res16, preferred_element_type=jnp.float32)  40.4 us
    dot_general x3, matrix products, run_group(): jnp.dot(samples, update.astype(jnp.bfloat16), preferred_element_type=jnp....  37.9 us
    dot_general x3, matrix products, run_group(): term = jnp.dot(inverse, grad_own, precision=lax.Precision.HIGHEST)  24.3 us
  transfers between devices with their start and end apart: 54, of which 54 were waited for; matrix products, arithmetic and copies ran while one was open for 4% of the time, Pallas kernels for 0%

profile of v1, /device:TPU:0, one launch (start us, length us, event | category | flops | bytes accessed | tf_op | source)
XLA Modules:
  0.0 1197.5 jit_solution(12678791152060580786)
XLA Ops:
  7.2 11.9 fusion.23
  19.2 83.5 %reduce-scatter.4.cloned.1.call-done = f32[256,128]{1,0:T(8,128)} async-done(((f32[4096,128]{1,0:T(8,128)}), f32[256,128]{1,0:T(8,128)}) %reduce-scatter.4.cloned.1.call-update) | async-done | bytes 131088 | tf_op jit(solution)/shard_map/reduce_scatter | solution.py:17
  110.8 123.0 %all-reduce.7.cloned.1.call-done = f32[4096,128]{0,1:T(8,128)} async-done(((f32[4096,128]{0,1:T(8,128)}), f32[4096,128]{0,1:T(8,128)}) %all-reduce.7.cloned.1.call-update) | async-done | bytes 2097168 | tf_op jit(solution)/shard_map/psum | solution.py:21
  256.5 8.6 collective-permute-done.2
  273.6 8.6 collective-permute-done.4
  282.2 8.9 collective-permute-done.5
  291.1 9.7 collective-permute-done.6
  344.4 9.0 collective-permute-done.12
  370.7 12.4 %convolution_bitcast_fusion.7 = f32[2048,128]{0,1:T(8,128)} fusion(bf16[2048,4096]{1,0:T(8,128)(2,1)} %param.3, f32[4096,128]{1,0:T(8,128)S(1)} %constant_dynamic-update-slice_fusion.32), kind=kOutput, calls=%fused_computation.16 | convolution fusion | flops 2148007936 | bytes 19922944 | tf_op jit(solution)/shard_map/dot_general | solution.py:36
  384.7 14.0 %all-reduce.9.cloned.1.call-done = f32[2048,128]{0,1:T(8,128)} async-done(((f32[2048,128]{0,1:T(8,128)}), f32[2048,128]{0,1:T(8,128)}) %all-reduce.9.cloned.1.call-update) | async-done | bytes 1048592 | tf_op jit(solution)/shard_map/psum | solution.py:37
  398.7 14.0 %convolution_bitcast_fusion.1 = f32[4096,128]{1,0:T(8,128)} fusion(bf16[2048,4096]{1,0:T(8,128)(2,1)} %param.3, f32[2048,128]{0,1:T(8,128)S(1)} %copy.21, f32[2048,128]{0,1:T(8,128)} %all-reduce.9.cloned.1.call-done), kind=kOutput, calls=%fused_computation.1 | convolution fusion | flops 2148270080 | bytes 20971520 | tf_op jit(solution)/shard_map/rb,rk->bk/dot_general | solution.py:14
  414.3 80.4 %reduce-scatter.6.cloned.1.call-done = f32[256,128]{1,0:T(8,128)} async-done(((f32[4096,128]{1,0:T(8,128)}), f32[256,128]{1,0:T(8,128)}) %reduce-scatter.6.cloned.1.call-update) | async-done | bytes 131088 | tf_op jit(solution)/shard_map/reduce_scatter | solution.py:17
  503.1 123.1 %all-reduce.11.cloned.1.call-done = f32[4096,128]{0,1:T(8,128)} async-done(((f32[4096,128]{0,1:T(8,128)}), f32[4096,128]{0,1:T(8,128)}) %all-reduce.11.cloned.1.call-update) | async-done | bytes 2097168 | tf_op jit(solution)/shard_map/psum | solution.py:21
  674.5 8.9 collective-permute-done.20
  683.4 9.8 collective-permute-done.21
  764.7 13.0 %convolution_bitcast_fusion.6 = f32[2048,128]{0,1:T(8,128)} fusion(bf16[2048,4096]{1,0:T(8,128)(2,1)} %param.3, f32[4096,128]{1,0:T(8,128)} %constant_dynamic-update-slice_fusion.16), kind=kOutput, calls=%fused_computation.15 | convolution fusion | flops 2148007936 | bytes 19922944 | tf_op jit(solution)/shard_map/dot_general | solution.py:36
  778.0 15.4 %all-reduce.13.cloned.1.call-done = f32[2048,128]{0,1:T(8,128)} async-done(((f32[2048,128]{0,1:T(8,128)}), f32[2048,128]{0,1:T(8,128)}) %all-reduce.13.cloned.1.call-update) | async-done | bytes 1048592 | tf_op jit(solution)/shard_map/psum | solution.py:37
  793.4 14.4 %convolution_bitcast_fusion = f32[4096,128]{1,0:T(8,128)} fusion(bf16[2048,4096]{1,0:T(8,128)(2,1)} %param.3, f32[2048,128]{0,1:T(8,128)} %all-reduce.13.cloned.1.call-done, f32[2048,128]{0,1:T(8,128)S(1)} %copy.21, f32[2048,128]{0,1:T(8,128)} %all-reduce.9.cloned.1.call-done), kind=kOutput, calls=%fused_computation | convolution fusion | flops 2148794368 | bytes 22020096 | tf_op jit(solution)/shard_map/rb,rk->bk/dot_general | solution.py:14
  811.0 78.7 %reduce-scatter.8.cloned.1.call-done = f32[256,128]{1,0:T(8,128)} async-done(((f32[4096,128]{1,0:T(8,128)}), f32[256,128]{1,0:T(8,128)}) %reduce-scatter.8.cloned.1.call-update) | async-done | bytes 131088 | tf_op jit(solution)/shard_map/reduce_scatter | solution.py:17
  898.2 123.0 %all-reduce.15.cloned.1.call-done = f32[4096,128]{0,1:T(8,128)} async-done(((f32[4096,128]{0,1:T(8,128)}), f32[4096,128]{0,1:T(8,128)}) %all-reduce.15.cloned.1.call-update) | async-done | bytes 2097168 | tf_op jit(solution)/shard_map/psum | solution.py:21
  1069.5 8.9 collective-permute-done.35
  1078.4 9.8 collective-permute-done.36
  1159.0 12.4 %convolution_bitcast_fusion.5 = f32[2048,128]{0,1:T(8,128)} fusion(bf16[2048,4096]{1,0:T(8,128)(2,1)} %param.3, f32[4096,128]{1,0:T(8,128)S(1)} %constant_dynamic-update-slice_fusion), kind=kOutput, calls=%fused_computation.14 | convolution fusion | flops 2148007936 | bytes 19922944 | tf_op jit(solution)/shard_map/dot_general | solution.py:36
  1174.5 12.5 %all-reduce.17.cloned.1.call-done = f32[2048,128]{0,1:T(8,128)} async-done(((f32[2048,128]{0,1:T(8,128)}), f32[2048,128]{0,1:T(8,128)}) %all-reduce.17.cloned.1.call-update) | async-done | bytes 1048592 | tf_op jit(solution)/shard_map/psum | solution.py:37
  (234 shorter events, 368.0 us)
Async XLA Ops:
  7.2 95.5 %reduce-scatter.4.cloned.1.call-start = ((), (), s32[]{:S(2)}) async-start(), calls=%async_computation.3 | async-start | bytes 2228224 | tf_op jit(solution)/shard_map/reduce_scatter | solution.py:17
  19.2 214.7 %all-reduce.7.cloned.1.call-start = ((), (), s32[]{:S(2)}) async-start(), calls=%async_computation.4 | async-start | bytes 4194304 | tf_op jit(solution)/shard_map/psum | solution.py:21
  110.8 287.9 %all-reduce.9.cloned.1.call-start = ((), (), s32[]{:S(2)}) async-start(), calls=%async_computation.5 | async-start | bytes 2097152 | tf_op jit(solution)/shard_map/psum | solution.py:37
  238.8 9.1 collective-permute-start
  282.2 8.9 collective-permute-start.5
  291.1 9.7 collective-permute-start.6
  300.8 9.1 collective-permute-start.7
  344.2 9.2 collective-permute-start.12
  383.1 111.6 %reduce-scatter.6.cloned.1.call-start = ((), (), s32[]{:S(2)}) async-start(), calls=%async_computation.6 | async-start | bytes 2228224 | tf_op jit(solution)/shard_map/reduce_scatter | solution.py:17
  412.8 213.5 %all-reduce.11.cloned.1.call-start = ((), (), s32[]{:S(2)}) async-start(), calls=%async_computation.7 | async-start | bytes 4194304 | tf_op jit(solution)/shard_map/psum | solution.py:21
  502.9 290.5 %all-reduce.13.cloned.1.call-start = ((), (), s32[]{:S(2)}) async-start(), calls=%async_computation.8 | async-start | bytes 2097152 | tf_op jit(solution)/shard_map/psum | solution.py:37
  631.2 9.1 collective-permute-start.15
  674.5 8.9 collective-permute-start.20
  683.4 9.8 collective-permute-start.21
  693.3 9.1 collective-permute-start.22
  711.1 8.9 collective-permute-start.24
  719.9 8.9 collective-permute-start.25
  777.7 112.0 %reduce-scatter.8.cloned.1.call-start = ((), (), s32[]{:S(2)}) async-start(), calls=%async_computation.9 | async-start | bytes 2228224 | tf_op jit(solution)/shard_map/reduce_scatter | solution.py:17
  807.8 213.4 %all-reduce.15.cloned.1.call-start = ((), (), s32[]{:S(2)}) async-start(), calls=%async_computation.10 | async-start | bytes 4194304 | tf_op jit(solution)/shard_map/psum | solution.py:21
  897.9 289.1 %all-reduce.17.cloned.1.call-start = ((), (), s32[]{:S(2)}) async-start(), calls=%async_computation.11 | async-start | bytes 2097152 | tf_op jit(solution)/shard_map/psum | solution.py:37
  1026.1 9.1 collective-permute-start.30
  1069.5 8.9 collective-permute-start.35
  1078.4 9.8 collective-permute-start.36
  1088.2 9.1 collective-permute-start.37
  (42 other events, 399.0 us)
Sparse Core Ops, SparseCore 0:
  19.3 83.3 reduce-scatter.3
  110.9 122.9 all-reduce.6
  383.2 15.4 all-reduce.8
  412.9 81.7 reduce-scatter.5
  503.0 123.1 all-reduce.10
  777.9 15.4 all-reduce.12
  807.9 81.7 reduce-scatter.7
  898.0 123.0 all-reduce.14
  1171.5 15.4 all-reduce.16
